TPU v7x, 32 devices: a whole 2x2x4 slice. The times are simulated.
32 devices in a mesh: ctx: 4 (over y, core), tp: 4 (over z), dp: 2 (over x).
Axes of the slice: x: 2, y: 2, z: 4, core: 2. Of those that a mesh axis runs over, the one named last changes fastest.
Arguments:
- tokens: bfloat16 [3072, 3584], P(('dp', 'ctx'), 'tp'), may hold values from -6 to 6
- expert_ids: int32 [3072, 8], P(('dp', 'ctx')), may hold values from 0 to 255, all different within a row; in each aligned block of 384 rows (0 to 383, 384 to 767, ...) at most 24 rows name the same one
- gate_codes: int32 [3072, 8], P(('dp', 'ctx')), may hold values from 1 to 32767
- up_weight: bfloat16 [4, 3584, 1024], P('ctx', 'tp', 'dp'), may hold values from -0.09375 to 0.09375
- down_weight: bfloat16 [4, 1024, 3584], P('ctx', 'dp', 'tp'), may hold values from -0.1875 to 0.1875
- cotangent: bfloat16 [3072, 3584], P(('dp', 'ctx'), 'tp'), may hold values from -6 to 6
Outputs:
- mixed: bfloat16 [3072, 3584], P(('dp', 'ctx'), 'tp')
- grad_tokens: bfloat16 [3072, 3584], P(('dp', 'ctx'), 'tp')
- grad_up: bfloat16 [4, 3584, 1024], P('ctx', 'tp', 'dp')
- grad_down: bfloat16 [4, 1024, 3584], P('ctx', 'dp', 'tp')
Inputs may be any that keep to these rules, and one draw needn't show every extreme that they name: `expert_ids`: each row names 8 different experts; among the 384 rows of one device no expert is named more than 24 times.
All inputs are finite; a program needn't handle non-finite values.
Results may differ from a plain program's by a relative error of at most 0.0066.
Values may be sent and summed in bfloat16 or wider, within the bound.
A program may use at most 64 MiB of HBM per device.

v0:
```python
import jax
import jax.numpy as jnp
from jax import lax
from jax.sharding import PartitionSpec as P


def place_slots(expert_ids, gate_codes, experts, capacity):
    rows_count, picks = expert_ids.shape
    flat_ids = expert_ids.reshape(-1)
    one_hot = (flat_ids[:, None] == jnp.arange(experts, dtype=jnp.int32)[None, :]).astype(jnp.int32)
    before = jnp.cumsum(one_hot, axis=0) - one_hot
    slot_rank = jnp.sum(before * one_hot, axis=1)
    inside = flat_ids < experts
    target = jnp.where(inside, flat_ids * capacity + slot_rank, experts * capacity)
    source = jnp.arange(rows_count * picks, dtype=jnp.int32) // picks
    slot_token = (
        jnp.full((experts * capacity,), rows_count, jnp.int32).at[target].set(source, mode="drop")
    )
    weights = gate_codes.reshape(-1).astype(jnp.float32) / 32768.0
    gate_slot = jnp.zeros((experts * capacity,), jnp.float32).at[target].set(weights, mode="drop")
    return (slot_token, gate_slot)


def silu_grad(values):
    sigma = jax.nn.sigmoid(values)
    return sigma * (1.0 + values * (1.0 - sigma))


def body(tokens, expert_ids, gate_codes, up_weight, down_weight, cotangent):
    sources = lax.axis_size("ctx")
    rows_count, features = tokens.shape
    capacity = rows_count // 16
    slot_token, gate_slot = place_slots(expert_ids, gate_codes, sources, capacity)
    padded_x = jnp.concatenate([tokens, jnp.zeros((1, features), tokens.dtype)], axis=0)
    outgoing = padded_x[slot_token].reshape(sources, capacity, features)
    arrived = lax.all_to_all(outgoing, "ctx", split_axis=0, concat_axis=0, tiled=True).reshape(
        sources * capacity, features
    )
    w_up, w_down = (
        lax.all_gather(up_weight[0], "dp", axis=1, tiled=True),
        lax.all_gather(down_weight[0], "dp", axis=0, tiled=True),
    )
    hidden = lax.psum(jnp.dot(arrived, w_up, preferred_element_type=jnp.float32), "tp")
    active = jax.nn.silu(hidden).astype(jnp.bfloat16)
    produced = jnp.dot(active, w_down, preferred_element_type=jnp.float32).astype(jnp.bfloat16)
    returned = lax.all_to_all(
        produced.reshape(sources, capacity, features),
        "ctx",
        split_axis=0,
        concat_axis=0,
        tiled=True,
    ).reshape(sources * capacity, features)
    mixed = (
        jnp.zeros((rows_count + 1, features), jnp.float32)
        .at[slot_token]
        .add(gate_slot[:, None] * returned.astype(jnp.float32))
    )
    mixed = mixed[:rows_count].astype(jnp.bfloat16)
    padded_c = jnp.concatenate([cotangent, jnp.zeros((1, features), cotangent.dtype)], axis=0)
    grad_send = (gate_slot[:, None] * padded_c[slot_token].astype(jnp.float32)).astype(jnp.bfloat16)
    grad_rows = lax.all_to_all(
        grad_send.reshape(sources, capacity, features),
        "ctx",
        split_axis=0,
        concat_axis=0,
        tiled=True,
    ).reshape(sources * capacity, features)
    contract_last = (((1,), (1,)), ((), ()))
    contract_first = (((0,), (0,)), ((), ()))
    grad_act = lax.psum(
        lax.dot_general(grad_rows, w_down, contract_last, preferred_element_type=jnp.float32), "tp"
    )
    grad_hid = (grad_act * silu_grad(hidden)).astype(jnp.bfloat16)
    grad_in = lax.dot_general(
        grad_hid, w_up, contract_last, preferred_element_type=jnp.float32
    ).astype(jnp.bfloat16)
    back_rows = lax.all_to_all(
        grad_in.reshape(sources, capacity, features), "ctx", split_axis=0, concat_axis=0, tiled=True
    ).reshape(sources * capacity, features)
    grad_tokens = (
        jnp.zeros((rows_count + 1, features), jnp.float32)
        .at[slot_token]
        .add(back_rows.astype(jnp.float32))
    )
    grad_tokens = grad_tokens[:rows_count].astype(jnp.bfloat16)
    part_up = lax.dot_general(arrived, grad_hid, contract_first, preferred_element_type=jnp.float32)
    part_down = lax.dot_general(
        active, grad_rows, contract_first, preferred_element_type=jnp.float32
    )
    grad_up, grad_down = (
        lax.psum_scatter(
            part_up.astype(jnp.bfloat16), "dp", scatter_dimension=1, tiled=True
        ).astype(jnp.float32),
        lax.psum_scatter(
            part_down.astype(jnp.bfloat16), "dp", scatter_dimension=0, tiled=True
        ).astype(jnp.float32),
    )
    return (
        mixed,
        grad_tokens,
        grad_up.astype(jnp.bfloat16)[None],
        grad_down.astype(jnp.bfloat16)[None],
    )


def solution(mesh):
    return jax.shard_map(
        body,
        mesh=mesh,
        in_specs=(
            P(("dp", "ctx"), "tp"),
            P(("dp", "ctx"), None),
            P(("dp", "ctx"), None),
            P("ctx", "tp", "dp"),
            P("ctx", "dp", "tp"),
            P(("dp", "ctx"), "tp"),
        ),
        out_specs=(
            P(("dp", "ctx"), "tp"),
            P(("dp", "ctx"), "tp"),
            P("ctx", "tp", "dp"),
            P("ctx", "dp", "tp"),
        ),
        check_vma=False,
    )
```

profile of v0, /device:TPU:0, one launch (start us, length us, event | category | flops | bytes accessed | tf_op | source)
XLA Modules:
  0.0 190.8 jit_solution(14327130908680088390)
XLA Ops:
  7.2 0.7 all-gather.5.cloned.1.call-update
  8.0 0.7 all-gather.7.cloned.1.call-update
  8.7 0.1 copy.12
  8.8 0.1 eq.29
  9.0 0.1 eq.25
  9.1 0.2 copy.10
  9.3 0.2 lt.35
  9.4 0.1 copy.11
  9.6 0.1 mul.53
  9.7 1.2 reduce-window.6
  10.9 0.2 slice_reduce_fusion
  11.1 0.2 reduce-window.9
  11.3 0.1 add_bitcast_fusion
  11.5 0.1 concatenate.6
  11.6 11.8 %scatter_custom_fusion = s32[96]{0:T(128)S(1)} fusion(s32[3072]{0:T(1024)S(1)} %bitcast.64, s32[3072]{0:T(1024)S(1)} %add_select_fusion, s32[]{:T(128)} %constant.17.clone.1), kind=kCustom, calls=%fused_computation.56 | custom fusion | bytes 388 | tf_op jit(solution)/shard_map/scatter | solution.py:17
  23.4 1.5 gather_fusion
  24.9 4.3 %all-to-all-start = ((bf16[4,24,896]{2,1,0:T(8,128)(2,1)}), bf16[4,24,896]{2,1,0:T(8,128)(2,1)S(1)}, u32[]{:S(2)}, u32[]{:S(2)}) async-start(bf16[4,24,896]{2,1,0:T(8,128)(2,1)} %bitcast.3), calls=%async_computation | async-start | bytes 344064 | tf_op jit(solution)/shard_map/all_to_all | solution.py:36
  29.1 0.1 copy.14
  29.3 0.1 reshape.139
  29.4 11.8 %scatter_custom_fusion.1 = f32[96]{0:T(128)S(1)} fusion(s32[3072]{0:T(1024)S(1)} %bitcast.65, f32[3072]{0:T(1024)S(1)} %reshape.139, f32[]{:T(128)} %constant.15.clone.1), kind=kCustom, calls=%fused_computation.54 | custom fusion | bytes 388 | tf_op jit(solution)/shard_map/scatter | solution.py:20
  41.2 0.1 mul.58
  41.3 0.1 concatenate.7
  41.3 0.8 gather_fusion.1
  42.1 0.8 fusion.19
  42.9 3.4 %all-to-all-start.2 = ((bf16[4,24,896]{2,1,0:T(8,128)(2,1)}), bf16[4,24,896]{2,1,0:T(8,128)(2,1)S(1)}, u32[]{:S(2)}, u32[]{:S(2)}) async-start(bf16[4,24,896]{2,1,0:T(8,128)(2,1)} %fusion.19), calls=%async_computation.2 | async-start | bytes 344064 | tf_op jit(solution)/shard_map/all_to_all | solution.py:61
  46.3 0.0 all-reduce.5.cloned.1.call-start
  46.3 2.7 %fusion.6 = f32[96,1024]{1,0:T(8,128)} fusion(bf16[96,896]{1,0:T(8,128)(2,1)S(1)} %bitcast.56, bf16[1,896,1024]{2,1,0:T(8,128)(2,1)} %all-gather.5.cloned.1.call-done), kind=kOutput, calls=%fused_computation.12 | convolution fusion | flops 176160768 | bytes 2400256 | tf_op jit(solution)/shard_map/dot_general | solution.py:43
  49.0 2.3 %all-to-all-done.2 = bf16[4,24,896]{2,1,0:T(8,128)(2,1)S(1)} async-done(((bf16[4,24,896]{2,1,0:T(8,128)(2,1)}), bf16[4,24,896]{2,1,0:T(8,128)(2,1)S(1)}, u32[]{:S(2)}, u32[]{:S(2)}) %all-to-all-start.2) | async-done | bytes 172064 | tf_op jit(solution)/shard_map/all_to_all | solution.py:61
  51.3 22.8 %all-gather.7.cloned.1.call-done = bf16[1,1024,896]{2,1,0:T(8,128)(2,1)} async-done(((bf16[1,512,896]{2,1,0:T(8,128)(2,1)}), bf16[1,1024,896]{2,1,0:T(8,128)(2,1)}) %all-gather.7.cloned.1.call-update) | async-done | bytes 1835024 | tf_op jit(solution)/shard_map/all_gather | solution.py:41
  74.1 2.9 %fusion = f32[96,1024]{1,0:T(8,128)} fusion(bf16[96,896]{1,0:T(8,128)(2,1)S(1)} %bitcast.58, bf16[1,1024,896]{2,1,0:T(8,128)(2,1)} %all-gather.7.cloned.1.call-done), kind=kOutput, calls=%fused_computation.6 | convolution fusion | flops 176160768 | bytes 2400256 | tf_op jit(solution)/shard_map/dot_general | solution.py:71
  77.1 0.0 reduce-scatter.5.cloned.1.call-start
  77.2 44.0 %all-reduce.5.cloned.1.call-done = (f32[96,1024]{1,0:T(8,128)}, f32[96,1024]{1,0:T(8,128)}) async-done(((f32[96,1024]{1,0:T(8,128)}, f32[96,1024]{1,0:T(8,128)}), (f32[96,1024]{1,0:T(8,128)}, f32[96,1024]{1,0:T(8,128)})) %all-reduce.5.cloned.1.call-update) | async-done | bytes 786448 | tf_op jit(solution)/shard_map/psum | solution.py:43
  121.2 3.0 %convolution_convert_fusion = bf16[1024,896]{1,0:T(8,128)(2,1)} fusion(bf16[96,896]{1,0:T(8,128)(2,1)S(1)} %bitcast.59, f32[96,1024]{1,0:T(8,128)} %get-tuple-element.4), kind=kOutput, calls=%fused_computation.14 | convolution fusion | flops 177569792 | bytes 2400256 | tf_op jit(solution)/shard_map/dot_general | solution.py:87
  124.2 0.0 reduce-scatter.3.cloned.1.call-start
  124.2 0.2 multiply_convert_fusion
  124.4 1.9 %convolution_convert_fusion.1 = bf16[896,1024]{1,0:T(8,128)(2,1)} fusion(bf16[96,896]{1,0:T(8,128)(2,1)S(1)} %bitcast.57, bf16[96,1024]{1,0:T(8,128)(2,1)S(1)} %multiply_convert_fusion), kind=kOutput, calls=%fused_computation.15 | convolution fusion | flops 177078272 | bytes 2203648 | tf_op jit(solution)/shard_map/dot_general | solution.py:86
  126.4 2.8 %fusion.11 = bf16[96,896]{1,0:T(8,128)(2,1)} fusion(bf16[1,1024,896]{2,1,0:T(8,128)(2,1)} %all-gather.7.cloned.1.call-done, f32[96,1024]{1,0:T(8,128)S(1)} %copy-done.1), kind=kOutput, calls=%fused_computation.19 | convolution fusion | flops 176738304 | bytes 2400256 | tf_op jit(solution)/shard_map/dot_general | solution.py:45
  129.1 3.4 %all-to-all-start.1 = ((bf16[4,24,896]{2,1,0:T(8,128)(2,1)}), bf16[4,24,896]{2,1,0:T(8,128)(2,1)S(1)}, u32[]{:S(2)}, u32[]{:S(2)}) async-start(bf16[4,24,896]{2,1,0:T(8,128)(2,1)} %bitcast.7), calls=%async_computation.1 | async-start | bytes 344064 | tf_op jit(solution)/shard_map/all_to_all | solution.py:46
  132.5 1.3 fusion.8
  133.8 3.7 %all-to-all-done.1 = bf16[4,24,896]{2,1,0:T(8,128)(2,1)S(1)} async-done(((bf16[4,24,896]{2,1,0:T(8,128)(2,1)}), bf16[4,24,896]{2,1,0:T(8,128)(2,1)S(1)}, u32[]{:S(2)}, u32[]{:S(2)}) %all-to-all-start.1) | async-done | bytes 172064 | tf_op jit(solution)/shard_map/all_to_all | solution.py:46
  137.5 3.3 %all-to-all-start.3 = ((bf16[4,24,896]{2,1,0:T(8,128)(2,1)}), bf16[4,24,896]{2,1,0:T(8,128)(2,1)S(1)}, u32[]{:S(2)}, u32[]{:S(2)}) async-start(bf16[4,24,896]{2,1,0:T(8,128)(2,1)} %bitcast.11), calls=%async_computation.3 | async-start | bytes 344064 | tf_op jit(solution)/shard_map/all_to_all | solution.py:77
  140.8 1.8 scatter_custom_fusion.2
  142.6 0.9 slice.29
  143.6 2.3 %all-to-all-done.3 = bf16[4,24,896]{2,1,0:T(8,128)(2,1)S(1)} async-done(((bf16[4,24,896]{2,1,0:T(8,128)(2,1)}), bf16[4,24,896]{2,1,0:T(8,128)(2,1)S(1)}, u32[]{:S(2)}, u32[]{:S(2)}) %all-to-all-start.3) | async-done | bytes 172064 | tf_op jit(solution)/shard_map/all_to_all | solution.py:77
  145.9 1.7 scatter_custom_fusion.3
  147.6 0.9 slice.28
  148.5 4.1 %reduce-scatter.5.cloned.1.call-done = bf16[512,896]{1,0:T(8,128)(2,1)} async-done(((bf16[1024,896]{1,0:T(8,128)(2,1)}), bf16[512,896]{1,0:T(8,128)(2,1)}) %reduce-scatter.5.cloned.1.call-update) | async-done | bytes 917520 | tf_op jit(solution)/shard_map/reduce_scatter | solution.py:94
  152.5 31.7 %reduce-scatter.3.cloned.1.call-done = bf16[896,512]{1,0:T(8,128)(2,1)} async-done(((bf16[896,1024]{1,0:T(8,128)(2,1)}), bf16[896,512]{1,0:T(8,128)(2,1)}) %reduce-scatter.3.cloned.1.call-update) | async-done | bytes 917520 | tf_op jit(solution)/shard_map/reduce_scatter | solution.py:91
  (30 shorter events, 0.3 us)
Async XLA Ops:
  7.2 1.5 copy-start.5
  7.2 4.3 %copy-start.2 = (bf16[384,896]{1,0:T(8,128)(2,1)S(1)}, bf16[384,896]{1,0:T(8,128)(2,1)}, u32[]{:S(2)}) copy-start(bf16[384,896]{1,0:T(8,128)(2,1)} %param.6) | copy-start | bytes 2064388
  7.2 39.1 %all-gather.5.cloned.1.call-start = ((), (), s32[]{:S(2)}) async-start(), calls=%async_computation.8 | async-start | bytes 2752512 | tf_op jit(solution)/shard_map/all_gather | solution.py:40
  7.9 66.2 %all-gather.7.cloned.1.call-start = ((), (), s32[]{:S(2)}) async-start(), calls=%async_computation.9 | async-start | bytes 2752512 | tf_op jit(solution)/shard_map/all_gather | solution.py:41
  9.7 19.4 %copy-start.6 = (s32[384,8]{0,1:T(8,128)S(1)}, s32[384,8]{0,1:T(8,128)}, u32[]{:S(2)}) copy-start(s32[384,8]{0,1:T(8,128)} %param.8) | copy-start | bytes 36868
  11.5 29.8 %copy-start.3 = (bf16[384,896]{1,0:T(8,128)(2,1)S(1)}, bf16[384,896]{1,0:T(8,128)(2,1)}, u32[]{:S(2)}) copy-start(bf16[384,896]{1,0:T(8,128)(2,1)} %param.11) | copy-start | bytes 2064388
  24.9 18.0 %all-to-all-start = ((bf16[4,24,896]{2,1,0:T(8,128)(2,1)}), bf16[4,24,896]{2,1,0:T(8,128)(2,1)S(1)}, u32[]{:S(2)}, u32[]{:S(2)}) async-start(bf16[4,24,896]{2,1,0:T(8,128)(2,1)} %bitcast.3), calls=%async_computation | async-start | bytes 344064 | tf_op jit(solution)/shard_map/all_to_all | solution.py:36
  42.9 8.4 %all-to-all-start.2 = ((bf16[4,24,896]{2,1,0:T(8,128)(2,1)}), bf16[4,24,896]{2,1,0:T(8,128)(2,1)S(1)}, u32[]{:S(2)}, u32[]{:S(2)}) async-start(bf16[4,24,896]{2,1,0:T(8,128)(2,1)} %fusion.19), calls=%async_computation.2 | async-start | bytes 344064 | tf_op jit(solution)/shard_map/all_to_all | solution.py:61
  46.3 74.9 %all-reduce.5.cloned.1.call-start = ((), (), s32[]{:S(2)}) async-start(), calls=%async_computation.10 | async-start | bytes 1572864 | tf_op jit(solution)/shard_map/psum | solution.py:43
  77.1 75.4 %reduce-scatter.5.cloned.1.call-start = ((), (), s32[]{:S(2)}) async-start(), calls=%async_computation.7 | async-start | bytes 2752512 | tf_op jit(solution)/shard_map/reduce_scatter | solution.py:94
  121.2 3.1 %copy-start.1 = (f32[96,1024]{1,0:T(8,128)S(1)}, f32[96,1024]{1,0:T(8,128)}, u32[]{:S(2)}) copy-start(f32[96,1024]{1,0:T(8,128)} %get-tuple-element.4) | copy-start | bytes 1179652
  121.2 3.1 %copy-start.4 = (f32[96,1024]{1,0:T(8,128)S(1)}, f32[96,1024]{1,0:T(8,128)}, u32[]{:S(2)}) copy-start(f32[96,1024]{1,0:T(8,128)} %get-tuple-element.5) | copy-start | bytes 1179652
  124.2 60.1 %reduce-scatter.3.cloned.1.call-start = ((), (), s32[]{:S(2)}) async-start(), calls=%async_computation.6 | async-start | bytes 2752512 | tf_op jit(solution)/shard_map/reduce_scatter | solution.py:91
  126.4 6.1 %copy-start = (bf16[1,896,1024]{2,1,0:T(8,128)(2,1)S(1)}, bf16[1,896,1024]{2,1,0:T(8,128)(2,1)}, u32[]{:S(2)}) copy-start(bf16[1,896,1024]{2,1,0:T(8,128)(2,1)} %all-gather.5.cloned.1.call-done) | copy-start | bytes 5505028
  129.1 8.4 %all-to-all-start.1 = ((bf16[4,24,896]{2,1,0:T(8,128)(2,1)}), bf16[4,24,896]{2,1,0:T(8,128)(2,1)S(1)}, u32[]{:S(2)}, u32[]{:S(2)}) async-start(bf16[4,24,896]{2,1,0:T(8,128)(2,1)} %bitcast.7), calls=%async_computation.1 | async-start | bytes 344064 | tf_op jit(solution)/shard_map/all_to_all | solution.py:46
  137.5 8.4 %all-to-all-start.3 = ((bf16[4,24,896]{2,1,0:T(8,128)(2,1)}), bf16[4,24,896]{2,1,0:T(8,128)(2,1)S(1)}, u32[]{:S(2)}, u32[]{:S(2)}) async-start(bf16[4,24,896]{2,1,0:T(8,128)(2,1)} %bitcast.11), calls=%async_computation.3 | async-start | bytes 344064 | tf_op jit(solution)/shard_map/all_to_all | solution.py:77
Sparse Core Ops, SparseCore 0:
  9.5 32.8 all-gather.4
  44.0 30.1 all-gather.6
  77.2 43.8 all-reduce.4
  124.3 28.2 reduce-scatter.4
  155.2 29.0 reduce-scatter.2
where the time goes:
time: 191 us
  waiting for transfers between devices  112 us (59%)
  local copies, waits for them, and re-layouts  29.3 us (15%)
  matrix products  14.6 us (8%)
  starting transfers between devices  14.5 us (8%)
  between operations  14.1 us (7%)
  other arithmetic  5.97 us (3%)
    psum x1, waiting for transfers between devices, body(): lax.psum(jnp.dot(arrived, w_up, preferred_element_type=jnp.float32), 'tp')  44 us
    reduce_scatter x1, waiting for transfers between devices, body(): lax.psum_scatter(part_up.astype(jnp.bfloat16), 'dp', scatter_dimension=1,...  31.7 us
    all_gather x1, waiting for transfers between devices, body(): lax.all_gather(down_weight[0], 'dp', axis=0, tiled=True)  22.8 us
    scatter x1, local copies, waits for them, and re-layouts, place_slots(): jnp.full((experts * capacity,), rows_count, jnp.int32).at[target]  11.8 us
    scatter x1, local copies, waits for them, and re-layouts, place_slots(): jnp.zeros((experts * capacity,), jnp.float32).at[target]  11.8 us
    all_to_all x1, starting transfers between devices, body(): lax.all_to_all(outgoing, 'ctx', split_axis=0, concat_axis=0, tiled=True)  4.26 us
    reduce_scatter x1, waiting for transfers between devices, body(): lax.psum_scatter(part_down.astype(jnp.bfloat16), 'dp', scatter_dimension=...  4.05 us
  transfers between devices with their start and end apart: 9, of which 7 were waited for; matrix products, arithmetic and copies ran while one was open for 23% of the time, Pallas kernels for 0%

commit v1 on v0

--- a/solution.py
+++ b/solution.py
@@ -40,7 +40,9 @@
         lax.all_gather(up_weight[0], "dp", axis=1, tiled=True),
         lax.all_gather(down_weight[0], "dp", axis=0, tiled=True),
     )
-    hidden = lax.psum(jnp.dot(arrived, w_up, preferred_element_type=jnp.float32), "tp")
+    own = jnp.dot(arrived, w_up, preferred_element_type=jnp.float32)
+    parts = lax.all_gather(own, "tp")
+    hidden = jnp.sum(parts, axis=0)
     active = jax.nn.silu(hidden).astype(jnp.bfloat16)
     produced = jnp.dot(active, w_down, preferred_element_type=jnp.float32).astype(jnp.bfloat16)
     returned = lax.all_to_all(

time: 191 us -> 223 us (1.17)
  waiting for transfers between devices: 112 us -> 134 us
  blocking collectives: 0 us -> 16.8 us
  starting transfers between devices: 14.5 us -> 6.96 us
    all_gather x0 -> x1, waiting for transfers between devices: none -> 36.2 us  [body(): parts = lax.all_gather(own, 'tp')]
    all_to_all x0 -> x2, blocking collectives: none -> 16.8 us  [the longest x1 9.24 us: body(): lax.all_to_all(outgoing, 'ctx', split_axis=0, concat_axis=0, tiled=True)]
    all_gather x1, waiting for transfers between devices: 22.8 us -> 8.25 us  [body(): lax.all_gather(down_weight[0], 'dp', axis=0, tiled=True)]
    psum x1, waiting for transfers between devices: 44 us -> 35 us  [body(): lax.psum(lax.dot_general(grad_rows, w_down, contract_last, preferred_elem...]
    all_gather x1, waiting for transfers between devices: 0.02 us -> 8.96 us  [body(): lax.all_gather(up_weight[0], 'dp', axis=1, tiled=True)]
    all_to_all x2 -> x0, starting transfers between devices: 7.62 us -> none  [the longest x1 4.26 us: body(): lax.all_to_all(outgoing, 'ctx', split_axis=0, concat_axis=0, tiled=True)]
    all_to_all x2 -> x0, waiting for transfers between devices: 2.27 us -> none  [the longest x1 2.27 us: body(): lax.all_to_all(grad_send.reshape(sources, capacity, features), 'ctx', spl...]
  transfers between devices with their start and end apart: 9 -> 8, of which waited for: 7 -> 8; matrix products, arithmetic and copies ran while one was open for 23% -> 23% of each run, Pallas kernels for 0% -> 0%
where the time goes in v1:
time: 223 us; the launch traced here: 222 us
  waiting for transfers between devices  134 us (60%)
  local copies, waits for them, and re-layouts  28.6 us (13%)
  blocking collectives  16.8 us (8%)
  between operations  14.4 us (6%)
  matrix products  13.6 us (6%)
  other arithmetic  7.85 us (4%)
  starting transfers between devices  6.96 us (3%)
    all_gather x1, waiting for transfers between devices, body(): parts = lax.all_gather(own, 'tp')  36.2 us
    psum x1, waiting for transfers between devices, body(): lax.psum(lax.dot_general(grad_rows, w_down, contract_last, preferred_elem...  35 us
    reduce_scatter x1, waiting for transfers between devices, body(): lax.psum_scatter(part_up.astype(jnp.bfloat16), 'dp', scatter_dimension=1,...  31.7 us
    scatter x1, local copies, waits for them, and re-layouts, place_slots(): jnp.full((experts * capacity,), rows_count, jnp.int32).at[target]  11.8 us
    scatter x1, local copies, waits for them, and re-layouts, place_slots(): jnp.zeros((experts * capacity,), jnp.float32).at[target]  11.8 us
    all_to_all x1, blocking collectives, body(): lax.all_to_all(outgoing, 'ctx', split_axis=0, concat_axis=0, tiled=True)  9.24 us
    all_gather x1, waiting for transfers between devices, body(): lax.all_gather(up_weight[0], 'dp', axis=1, tiled=True)  8.96 us
    all_gather x1, waiting for transfers between devices, body(): lax.all_gather(down_weight[0], 'dp', axis=0, tiled=True)  8.25 us
  transfers between devices with their start and end apart: 8, of which 8 were waited for; matrix products, arithmetic and copies ran while one was open for 23% of the time, Pallas kernels for 0%

profile of v1, /device:TPU:0, one launch (start us, length us, event | category | flops | bytes accessed | tf_op | source)
XLA Modules:
  0.0 222.0 jit_solution(7982316212200654201)
XLA Ops:
  7.2 0.7 all-gather.7.cloned.1.call-update
  8.0 0.7 all-gather.11.cloned.1.call-update
  8.7 0.1 copy.12
  8.9 0.1 eq.29
  9.0 0.1 eq.25
  9.1 0.2 copy.10
  9.3 0.2 lt.35
  9.5 0.1 copy.11
  9.6 0.1 mul.53
  9.8 1.2 reduce-window.6
  10.9 0.2 slice_reduce_fusion
  11.1 0.2 reduce-window.9
  11.4 0.1 concatenate.6
  11.4 0.1 add_bitcast_fusion
  11.6 11.8 %scatter_custom_fusion = s32[96]{0:T(128)S(1)} fusion(s32[3072]{0:T(1024)S(1)} %bitcast.67, s32[3072]{0:T(1024)S(1)} %add_select_fusion, s32[]{:T(128)} %constant.16.clone.1), kind=kCustom, calls=%fused_computation.56 | custom fusion | bytes 388 | tf_op jit(solution)/shard_map/scatter | solution.py:17
  23.4 0.8 gather_fusion
  24.2 9.2 %all_to_all.20 = bf16[4,24,896]{2,1,0:T(8,128)(2,1)S(1)} all-to-all(bf16[4,24,896]{2,1,0:T(8,128)(2,1)S(1)} %bitcast.65), channel_id=1, replica_groups=mesh['ctx'=4,'tp'=4,'dp'=2] {'ctx'}, dimensions={0} | all-to-all | bytes 344064 | tf_op jit(solution)/shard_map/all_to_all | solution.py:36
  33.5 9.0 %all-gather.7.cloned.1.call-done = bf16[1,896,1024]{2,1,0:T(8,128)(2,1)} async-done(((bf16[1,896,512]{2,1,0:T(8,128)(2,1)}), bf16[1,896,1024]{2,1,0:T(8,128)(2,1)}) %all-gather.7.cloned.1.call-update) | async-done | bytes 1835024 | tf_op jit(solution)/shard_map/all_gather | solution.py:40
  42.4 2.7 %fusion.6 = f32[96,1024]{1,0:T(8,128)} fusion(bf16[96,896]{1,0:T(8,128)(2,1)S(1)} %bitcast.58, bf16[1,896,1024]{2,1,0:T(8,128)(2,1)} %all-gather.7.cloned.1.call-done), kind=kOutput, calls=%fused_computation.12 | convolution fusion | flops 176160768 | bytes 2400256 | tf_op jit(solution)/shard_map/dot_general | solution.py:43
  45.2 0.0 all-reduce.4.cloned.1.call-start
  45.2 0.1 copy.14
  45.4 0.1 reshape.139
  45.5 11.8 %scatter_custom_fusion.1 = f32[96]{0:T(128)S(1)} fusion(s32[3072]{0:T(1024)S(1)} %bitcast.68, f32[3072]{0:T(1024)S(1)} %reshape.139, f32[]{:T(128)} %constant.15.clone.1), kind=kCustom, calls=%fused_computation.54 | custom fusion | bytes 388 | tf_op jit(solution)/shard_map/scatter | solution.py:20
  57.3 0.1 mul.58
  57.4 0.1 concatenate.7
  57.4 0.8 gather_fusion.1
  58.2 0.1 fusion.19
  58.3 7.6 %all_to_all.21 = bf16[4,24,896]{2,1,0:T(8,128)(2,1)S(1)} all-to-all(bf16[4,24,896]{2,1,0:T(8,128)(2,1)S(1)} %fusion.19), channel_id=1, replica_groups=mesh['ctx'=4,'tp'=4,'dp'=2] {'ctx'}, dimensions={0} | all-to-all | bytes 344064 | tf_op jit(solution)/shard_map/all_to_all | solution.py:63
  65.9 8.2 %all-gather.11.cloned.1.call-done = bf16[1,1024,896]{2,1,0:T(8,128)(2,1)} async-done(((bf16[1,512,896]{2,1,0:T(8,128)(2,1)}), bf16[1,1024,896]{2,1,0:T(8,128)(2,1)}) %all-gather.11.cloned.1.call-update) | async-done | bytes 1835024 | tf_op jit(solution)/shard_map/all_gather | solution.py:41
  74.1 2.9 %fusion = f32[96,1024]{1,0:T(8,128)} fusion(bf16[96,896]{1,0:T(8,128)(2,1)S(1)} %bitcast.60, bf16[1,1024,896]{2,1,0:T(8,128)(2,1)} %all-gather.11.cloned.1.call-done), kind=kOutput, calls=%fused_computation.6 | convolution fusion | flops 176160768 | bytes 2400256 | tf_op jit(solution)/shard_map/dot_general | solution.py:73
  77.2 36.2 %all-gather.9.cloned.1.call-done = f32[384,1024]{1,0:T(8,128)} async-done(((f32[96,1024]{1,0:T(8,128)}), f32[384,1024]{1,0:T(8,128)}) %all-gather.9.cloned.1.call-update) | async-done | bytes 1572880 | tf_op jit(solution)/shard_map/all_gather | solution.py:44
  113.4 1.6 reduce_sum.22
  114.9 2.0 convolution_convert_fusion
  116.9 35.0 %all-reduce.4.cloned.1.call-done = f32[96,1024]{1,0:T(8,128)} async-done(((f32[96,1024]{1,0:T(8,128)}), f32[96,1024]{1,0:T(8,128)}) %all-reduce.4.cloned.1.call-update) | async-done | bytes 393232 | tf_op jit(solution)/shard_map/psum | solution.py:72
  152.0 1.1 multiply_convert_fusion
  153.1 2.0 convolution_convert_fusion.1
  155.1 2.8 %fusion.11 = bf16[96,896]{1,0:T(8,128)(2,1)} fusion(bf16[1,1024,896]{2,1,0:T(8,128)(2,1)} %all-gather.11.cloned.1.call-done, f32[96,1024]{1,0:T(8,128)S(1)} %reduce_sum.22), kind=kOutput, calls=%fused_computation.19 | convolution fusion | flops 176738304 | bytes 2400256 | tf_op jit(solution)/shard_map/dot_general | solution.py:47
  157.9 3.4 %all-to-all-start.1 = ((bf16[4,24,896]{2,1,0:T(8,128)(2,1)}), bf16[4,24,896]{2,1,0:T(8,128)(2,1)S(1)}, u32[]{:S(2)}, u32[]{:S(2)}) async-start(bf16[4,24,896]{2,1,0:T(8,128)(2,1)} %bitcast.8), calls=%async_computation.1 | async-start | bytes 344064 | tf_op jit(solution)/shard_map/all_to_all | solution.py:48
  161.3 1.3 fusion.8
  162.6 3.6 %all-to-all-done.1 = bf16[4,24,896]{2,1,0:T(8,128)(2,1)S(1)} async-done(((bf16[4,24,896]{2,1,0:T(8,128)(2,1)}), bf16[4,24,896]{2,1,0:T(8,128)(2,1)S(1)}, u32[]{:S(2)}, u32[]{:S(2)}) %all-to-all-start.1) | async-done | bytes 172064 | tf_op jit(solution)/shard_map/all_to_all | solution.py:48
  166.3 3.4 %all-to-all-start.3 = ((bf16[4,24,896]{2,1,0:T(8,128)(2,1)}), bf16[4,24,896]{2,1,0:T(8,128)(2,1)S(1)}, u32[]{:S(2)}, u32[]{:S(2)}) async-start(bf16[4,24,896]{2,1,0:T(8,128)(2,1)} %bitcast.12), calls=%async_computation.3 | async-start | bytes 344064 | tf_op jit(solution)/shard_map/all_to_all | solution.py:79
  169.6 1.8 scatter_custom_fusion.2
  171.4 0.9 slice.29
  172.3 2.3 %all-to-all-done.3 = bf16[4,24,896]{2,1,0:T(8,128)(2,1)S(1)} async-done(((bf16[4,24,896]{2,1,0:T(8,128)(2,1)}), bf16[4,24,896]{2,1,0:T(8,128)(2,1)S(1)}, u32[]{:S(2)}, u32[]{:S(2)}) %all-to-all-start.3) | async-done | bytes 172064 | tf_op jit(solution)/shard_map/all_to_all | solution.py:79
  174.6 1.7 scatter_custom_fusion.3
  176.3 0.9 slice.28
  177.3 6.2 %reduce-scatter.5.cloned.1.call-done = bf16[512,896]{1,0:T(8,128)(2,1)} async-done(((bf16[1024,896]{1,0:T(8,128)(2,1)}), bf16[512,896]{1,0:T(8,128)(2,1)}) %reduce-scatter.5.cloned.1.call-update) | async-done | bytes 917520 | tf_op jit(solution)/shard_map/reduce_scatter | solution.py:96
  183.5 31.7 %reduce-scatter.3.cloned.1.call-done = bf16[896,512]{1,0:T(8,128)(2,1)} async-done(((bf16[896,1024]{1,0:T(8,128)(2,1)}), bf16[896,512]{1,0:T(8,128)(2,1)}) %reduce-scatter.3.cloned.1.call-update) | async-done | bytes 917520 | tf_op jit(solution)/shard_map/reduce_scatter | solution.py:93
  (28 shorter events, 0.4 us)
Async XLA Ops:
  7.2 1.6 copy-start.3
  7.2 4.2 %copy-start.1 = (bf16[384,896]{1,0:T(8,128)(2,1)S(1)}, bf16[384,896]{1,0:T(8,128)(2,1)}, u32[]{:S(2)}) copy-start(bf16[384,896]{1,0:T(8,128)(2,1)} %param.6) | copy-start | bytes 2064388
  7.2 35.2 %all-gather.7.cloned.1.call-start = ((), (), s32[]{:S(2)}) async-start(), calls=%async_computation.9 | async-start | bytes 2752512 | tf_op jit(solution)/shard_map/all_gather | solution.py:40
  7.9 66.2 %all-gather.11.cloned.1.call-start = ((), (), s32[]{:S(2)}) async-start(), calls=%async_computation.11 | async-start | bytes 2752512 | tf_op jit(solution)/shard_map/all_gather | solution.py:41
  8.7 104.7 %all-gather.9.cloned.1.call-start = ((), (), s32[]{:S(2)}) async-start(), calls=%async_computation.10 | async-start | bytes 1966080 | tf_op jit(solution)/shard_map/all_gather | solution.py:44
  24.2 21.0 %copy-start.4 = (s32[384,8]{0,1:T(8,128)S(1)}, s32[384,8]{0,1:T(8,128)}, u32[]{:S(2)}) copy-start(s32[384,8]{0,1:T(8,128)} %param.8) | copy-start | bytes 36868
  24.2 33.1 %copy-start.2 = (bf16[384,896]{1,0:T(8,128)(2,1)S(1)}, bf16[384,896]{1,0:T(8,128)(2,1)}, u32[]{:S(2)}) copy-start(bf16[384,896]{1,0:T(8,128)(2,1)} %param.11) | copy-start | bytes 2064388
  45.2 106.8 %all-reduce.4.cloned.1.call-start = ((), (), s32[]{:S(2)}) async-start(), calls=%async_computation.6 | async-start | bytes 786432 | tf_op jit(solution)/shard_map/psum | solution.py:72
  77.1 106.4 %reduce-scatter.5.cloned.1.call-start = ((), (), s32[]{:S(2)}) async-start(), calls=%async_computation.8 | async-start | bytes 2752512 | tf_op jit(solution)/shard_map/reduce_scatter | solution.py:96
  116.9 98.3 %reduce-scatter.3.cloned.1.call-start = ((), (), s32[]{:S(2)}) async-start(), calls=%async_computation.7 | async-start | bytes 2752512 | tf_op jit(solution)/shard_map/reduce_scatter | solution.py:93
  155.1 6.1 %copy-start = (bf16[1,896,1024]{2,1,0:T(8,128)(2,1)S(1)}, bf16[1,896,1024]{2,1,0:T(8,128)(2,1)}, u32[]{:S(2)}) copy-start(bf16[1,896,1024]{2,1,0:T(8,128)(2,1)} %all-gather.7.cloned.1.call-done) | copy-start | bytes 5505028
  157.9 8.4 %all-to-all-start.1 = ((bf16[4,24,896]{2,1,0:T(8,128)(2,1)}), bf16[4,24,896]{2,1,0:T(8,128)(2,1)S(1)}, u32[]{:S(2)}, u32[]{:S(2)}) async-start(bf16[4,24,896]{2,1,0:T(8,128)(2,1)} %bitcast.8), calls=%async_computation.1 | async-start | bytes 344064 | tf_op jit(solution)/shard_map/all_to_all | solution.py:48
  166.3 8.4 %all-to-all-start.3 = ((bf16[4,24,896]{2,1,0:T(8,128)(2,1)}), bf16[4,24,896]{2,1,0:T(8,128)(2,1)S(1)}, u32[]{:S(2)}, u32[]{:S(2)}) async-start(bf16[4,24,896]{2,1,0:T(8,128)(2,1)} %bitcast.12), calls=%async_computation.3 | async-start | bytes 344064 | tf_op jit(solution)/shard_map/all_to_all | solution.py:79
Sparse Core Ops, SparseCore 0:
  9.5 32.8 all-gather.6
  44.0 30.1 all-gather.10
  76.3 37.0 all-gather.8
  116.1 35.8 all-reduce.3
  154.7 28.7 reduce-scatter.4
  186.1 28.9 reduce-scatter.2
